TPU v7x, 128 devices: a whole 4x4x4 slice. The times are simulated.
128 devices in a mesh: req: 16 (over z, x_hi, core), mdl: 8 (over x_lo, y).
Axes of the slice: x: 4 (x_hi: 2, x_lo: 2; x = x_hi * 2 + x_lo), y: 4, z: 4, core: 2. Of those that a mesh axis runs over, the one named last changes fastest.
Arguments:
- tokens: bfloat16 [16384, 2048], P('req'), may hold values from -6 to 6
- doc_ids: int32 [16384], P('req'), may hold values from 0 to 16383, as said below
- positions: int32 [16384], P('req'), may hold values from 0 to 1023, as said below
- attn_gain: float32 [2048], replicated, may hold values from 0.5 to 1.5
- mlp_gain: float32 [2048], replicated, may hold values from 0.5 to 1.5
- q_gain: float32 [128], replicated, may hold values from 0.5 to 48
- key_norm_gain: float32 [128], replicated, may hold values from 0.5 to 1.5
- q_weight: float32 [2048, 2048], P('req', 'mdl'), may hold values from -0.125 to 0.125
- key_matrix: float32 [2048, 1024], P('req', 'mdl'), may hold values from -0.125 to 0.125
- value_matrix: float32 [2048, 1024], P('req', 'mdl'), may hold values from -0.125 to 0.125
- o_weight: float32 [2048, 2048], P('mdl', 'req'), may hold values from -0.125 to 0.125
- gate_weight: float32 [2048, 6144], P('mdl', 'req'), may hold values from -0.125 to 0.125
- up_weight: float32 [2048, 6144], P('mdl', 'req'), may hold values from -0.125 to 0.125
- down_weight: float32 [6144, 2048], P('req', 'mdl'), may hold values from -0.078125 to 0.078125
Outputs:
- layer_out: bfloat16 [16384, 2048], P(('req', 'mdl'))
- key_value_cache: bfloat16 [2, 16384, 1024], P(None, 'req', 'mdl')
Inputs may be any that keep to these rules, and one draw needn't show every extreme that they name: `doc_ids`: A row's prompt number is the index of its prompt's first row among all packed rows, so it never falls along the rows; a prompt holds at most 1024 rows, every aligned block of 1024 rows has a prompt start in its second half, every block but the first begins inside the prompt that the block before it ends with, and the last row starts a prompt. `positions`: positions count from 0 at each prompt's first row.
All inputs are finite; a program needn't handle non-finite values.
Results may differ from a plain program's by a relative error of at most 0.02.
The roundings to bfloat16 on the way count: a program that leaves them out, or rounds other values in their place, can miss the bound.
Values may be sent and summed in bfloat16 or wider, within the bound.
No kernel may reach another device: no remote copies, remote signals or barrier semaphores. Data moves between devices by JAX's collectives and lax.ppermute only.
A program may use at most 128 MiB of HBM per device.

v0:
```python
import math
import jax
import jax.numpy as jnp
from jax import lax
from jax.sharding import PartitionSpec as P

HEAD_SIZE = 128


def passed_along(block, axis, distance):
    devices = range(lax.axis_size(axis))
    route = [(i - distance, i) for i in devices if i - distance in devices]
    return lax.ppermute(block, axis, route)


def root_mean_scale(values, gain):
    return values * lax.rsqrt(jnp.mean(values * values, axis=-1, keepdims=True) + 1e-06) * gain


def apply_rotary(tensor, position):
    half = tensor.shape[-1] // 2
    freq = jnp.exp(
        jnp.arange(half, dtype=jnp.float32) * (-2.0 * math.log(1000000.0) / tensor.shape[-1])
    )
    angle = position.astype(jnp.float32)[:, None] * freq[None, :]
    cosine = jnp.cos(angle)[:, None, :]
    sine = jnp.sin(angle)[:, None, :]
    front = tensor[..., :half]
    back = tensor[..., half:]
    return jnp.concatenate([front * cosine - back * sine, back * cosine + front * sine], axis=-1)


def per_device(
    tokens,
    doc_ids,
    positions,
    attn_gain,
    mlp_gain,
    q_gain,
    key_norm_gain,
    q_weight,
    key_matrix,
    value_matrix,
    o_weight,
    gate_weight,
    up_weight,
    down_weight,
):
    rows_here = tokens.shape[0]
    normed = root_mean_scale(tokens.astype(jnp.float32), attn_gain).astype(jnp.bfloat16)
    query_cols = q_weight.shape[1]
    kv_cols = key_matrix.shape[1]
    pieces = (
        lax.all_gather(q_weight.astype(jnp.bfloat16), "req", axis=0, tiled=True),
        lax.all_gather(key_matrix.astype(jnp.bfloat16), "req", axis=0, tiled=True),
        lax.all_gather(value_matrix.astype(jnp.bfloat16), "req", axis=0, tiled=True),
    )
    query_raw, unnormed_keys, unnormed_values = tuple(
        (jnp.dot(normed, piece, preferred_element_type=jnp.float32) for piece in pieces)
    )
    q_heads = query_cols // HEAD_SIZE
    kv_heads = kv_cols // HEAD_SIZE
    head_groups = q_heads // kv_heads
    query_rows = apply_rotary(
        root_mean_scale(query_raw.reshape(rows_here, q_heads, HEAD_SIZE), q_gain), positions
    ).astype(jnp.bfloat16)
    rotated_keys = (
        apply_rotary(
            root_mean_scale(unnormed_keys.reshape(rows_here, kv_heads, HEAD_SIZE), key_norm_gain),
            positions,
        )
        .astype(jnp.bfloat16)
        .reshape(rows_here, kv_cols)
    )
    projected_values = unnormed_values.astype(jnp.bfloat16)
    key_value_cache = jnp.stack([rotated_keys, projected_values])
    prior_keys, prior_values = passed_along((rotated_keys, projected_values), "req", 1)
    all_keys = jnp.concatenate([prior_keys, rotated_keys], axis=0).reshape(-1, kv_heads, HEAD_SIZE)
    all_values = jnp.concatenate([prior_values, projected_values], axis=0).reshape(
        -1, kv_heads, HEAD_SIZE
    )
    prior_index = jnp.arange(prior_keys.shape[0], dtype=jnp.int32)
    prior_live = prior_index >= rows_here - positions[0]
    grouped_queries = query_rows.reshape(rows_here, kv_heads, head_groups, HEAD_SIZE)
    block_rows = min(512, rows_here)
    scale = HEAD_SIZE ** (-0.5)
    outputs = []
    for block_index in range(rows_here // block_rows):
        lower = block_index * block_rows
        block_q = grouped_queries[lower : lower + block_rows]
        block_doc = doc_ids[lower : lower + block_rows]
        block_pos = positions[lower : lower + block_rows]
        scores = (
            jnp.einsum("qkrd,skd->krqs", block_q, all_keys, preferred_element_type=jnp.float32)
            * scale
        )
        earlier = (block_doc == doc_ids[0])[:, None] & prior_live[None, :]
        current = (doc_ids[None, :] == block_doc[:, None]) & (
            positions[None, :] <= block_pos[:, None]
        )
        allowed = jnp.concatenate([earlier, current], axis=1)
        scores = jnp.where(allowed[None, None], scores, -jnp.inf)
        top = jnp.max(scores, axis=-1, keepdims=True)
        expo = jnp.exp(scores - top)
        probs = (expo / jnp.sum(expo, axis=-1, keepdims=True)).astype(jnp.bfloat16)
        context_block = jnp.einsum(
            "krqs,skd->qkrd", probs, all_values, preferred_element_type=jnp.float32
        )
        outputs.append(context_block.astype(jnp.bfloat16).reshape(block_rows, q_heads * HEAD_SIZE))
    context = jnp.concatenate(outputs, axis=0)
    head_terms = jnp.dot(
        context,
        lax.all_gather(o_weight.astype(jnp.bfloat16), "req", axis=1, tiled=True),
        preferred_element_type=jnp.float32,
    )
    attn_rows = lax.psum_scatter(
        head_terms.astype(jnp.bfloat16), "mdl", scatter_dimension=0, tiled=True
    ).astype(jnp.float32)
    share = rows_here // lax.axis_size("mdl")
    own_rows = lax.dynamic_slice_in_dim(tokens, lax.axis_index("mdl") * share, share, 0)
    resid = lax.optimization_barrier(
        (own_rows.astype(jnp.float32) + attn_rows).astype(jnp.bfloat16)
    ).astype(jnp.float32)
    mlp_in = root_mean_scale(resid, mlp_gain).astype(jnp.bfloat16)
    gate_local = gate_weight.astype(jnp.bfloat16)
    up_local = up_weight.astype(jnp.bfloat16)
    down_local = down_weight.astype(jnp.bfloat16)
    gate_whole, up_whole = (
        lax.all_gather(gate_local, "req", axis=1, tiled=True),
        lax.all_gather(up_local, "req", axis=1, tiled=True),
    )
    down_whole = lax.all_gather(down_local, "req", axis=0, tiled=True)
    gate_server, up_server = (
        lax.all_to_all(gate_whole, "mdl", split_axis=1, concat_axis=0, tiled=True),
        lax.all_to_all(up_whole, "mdl", split_axis=1, concat_axis=0, tiled=True),
    )
    down_server = lax.all_to_all(down_whole, "mdl", split_axis=0, concat_axis=1, tiled=True)
    piece = lax.all_gather(mlp_in, "mdl", axis=0, tiled=True)
    gate = jnp.dot(piece, gate_server, preferred_element_type=jnp.float32)
    upper = jnp.dot(piece, up_server, preferred_element_type=jnp.float32)
    hidden = (jax.nn.silu(gate) * upper).astype(jnp.bfloat16)
    unit_terms = jnp.dot(hidden, down_server, preferred_element_type=jnp.float32)
    mlp_rows = lax.psum_scatter(
        unit_terms.astype(jnp.bfloat16), "mdl", scatter_dimension=0, tiled=True
    ).astype(jnp.float32)
    layer_out = (resid + mlp_rows).astype(jnp.bfloat16)
    return (layer_out, key_value_cache)


def solution(mesh):
    in_specs = (
        P("req", None),
        P("req"),
        P("req"),
        P(),
        P(),
        P(),
        P(),
        P("req", "mdl"),
        P("req", "mdl"),
        P("req", "mdl"),
        P("mdl", "req"),
        P("mdl", "req"),
        P("mdl", "req"),
        P("req", "mdl"),
    )
    out_specs = (P(("req", "mdl"), None), P(None, "req", "mdl"))
    return jax.shard_map(
        per_device, mesh=mesh, in_specs=in_specs, out_specs=out_specs, check_vma=False
    )
```

profile of v0, /device:TPU:1, one launch (start us, length us, event | category | flops | bytes accessed | tf_op | source)
XLA Modules:
  0.0 521.2 jit_solution(16136902884525856238)
XLA Ops:
  7.2 1.5 convert_element_type.107
  8.8 0.0 all-gather.9.cloned.1.call-start
  8.8 1.5 convert_element_type.116
  10.4 0.0 all-gather.13.cloned.1.call-start
  10.5 3.2 fusion
  13.7 0.2 copy-done
  13.9 1.0 fusion.2
  15.0 30.4 %all_gather.25 = bf16[2048,128]{1,0:T(8,128)(2,1)S(1)} all-gather(bf16[128,128]{1,0:T(8,128)(2,1)S(1)} %convert_element_type.105), channel_id=1, replica_groups=mesh['req'=16,'mdl'=8] {'req'}, dimensions={0}, use_global_device_ids=true | all-gather | bytes 557056 | tf_op jit(solution)/shard_map/all_gather | solution.py:55
  45.4 1.5 multiply_reduce_fusion.1
  46.9 0.2 copy.28
  47.2 0.2 multiply_bitcast_fusion
  47.4 2.4 fusion.26
  49.8 0.7 copy-done.4
  50.5 0.8 pad_maximum_fusion.3
  51.4 1.9 collective-permute-start.1
  53.3 23.4 %all_gather.24 = bf16[2048,128]{1,0:T(8,128)(2,1)S(1)} all-gather(bf16[128,128]{1,0:T(8,128)(2,1)S(1)} %convert_element_type.103), channel_id=1, replica_groups=mesh['req'=16,'mdl'=8] {'req'}, dimensions={0}, use_global_device_ids=true | all-gather | bytes 557056 | tf_op jit(solution)/shard_map/all_gather | solution.py:56
  76.7 4.1 convolution_convert_fusion.2
  80.9 3.5 collective-permute-start
  84.4 0.8 copy.34
  85.2 0.2 reduce-scatter.3.cloned.1.call-start
  85.5 0.5 slice.40
  86.0 0.5 slice.41
  86.5 3.0 multiply_cosine_fusion
  89.5 0.6 broadcast_compare_fusion.1
  90.8 0.5 broadcast_and_fusion.1
  91.3 1.2 compare_and_fusion.1
  92.5 0.8 pad_add_fusion
  93.3 4.8 multiply_reduce_fusion
  98.1 1.5 copy.29
  99.7 0.3 multiply_multiply_fusion
  100.1 1.7 subtract_convert_fusion
  101.8 2.9 fusion.5
  104.7 2.9 fusion.6
  107.6 2.0 fusion.3
  109.6 2.2 fusion.4
  111.8 3.9 fusion.11
  115.7 3.9 fusion.14
  119.7 4.5 convolution_convert_fusion
  124.2 0.0 all-gather.15.cloned.1.call-start
  124.3 0.8 copy.36
  125.1 0.0 all-gather.17.cloned.1.call-start
  125.2 0.7 convert_element_type.125
  125.9 31.1 %all-gather.13.cloned.1.call-done = bf16[256,6144]{0,1:T(8,128)(2,1)} async-done(((bf16[256,384]{0,1:T(8,128)(2,1)}), bf16[256,6144]{0,1:T(8,128)(2,1)}) %all-gather.13.cloned.1.call-update) | async-done | bytes 3145744 | tf_op jit(solution)/shard_map/all_gather | solution.py:129
  157.0 4.1 all-to-all-start
  161.2 81.4 %reduce-scatter.3.cloned.1.call-done = bf16[128,2048]{1,0:T(8,128)(2,1)} async-done(((bf16[1024,2048]{1,0:T(8,128)(2,1)}), bf16[128,2048]{1,0:T(8,128)(2,1)}) %reduce-scatter.3.cloned.1.call-update) | async-done | bytes 524304 | tf_op jit(solution)/shard_map/reduce_scatter | solution.py:116
  242.6 1.3 add_convert_fusion
  243.9 0.2 fusion.17
  244.1 0.6 copy-done.2
  244.7 1.0 fusion.19
  245.7 49.2 %all-gather.15.cloned.1.call-done = bf16[256,6144]{0,1:T(8,128)(2,1)} async-done(((bf16[256,384]{0,1:T(8,128)(2,1)}), bf16[256,6144]{0,1:T(8,128)(2,1)}) %all-gather.15.cloned.1.call-update) | async-done | bytes 3145744 | tf_op jit(solution)/shard_map/all_gather | solution.py:130
  295.0 4.5 all-to-all-start.1
  299.5 54.8 %all-gather.17.cloned.1.call-done = bf16[6144,256]{1,0:T(8,128)(2,1)} async-done(((bf16[384,256]{1,0:T(8,128)(2,1)}), bf16[6144,256]{1,0:T(8,128)(2,1)}) %all-gather.17.cloned.1.call-update) | async-done | bytes 3145744 | tf_op jit(solution)/shard_map/all_gather | solution.py:132
  354.2 4.6 all-to-all-start.2
  358.9 3.1 copy.35
  362.0 3.3 copy.37
  365.2 54.4 %all-to-all-done.2 = bf16[8,768,256]{2,1,0:T(8,128)(2,1)} async-done(((bf16[8,768,256]{2,1,0:T(8,128)(2,1)}), bf16[8,768,256]{2,1,0:T(8,128)(2,1)}, u32[]{:S(2)}, u32[]{:S(2)}) %all-to-all-start.2) | async-done | bytes 3145760 | tf_op jit(solution)/shard_map/all_to_all | solution.py:137
  419.6 4.7 copy.38
  424.3 15.7 %all-gather.11.cloned.1.call-done = bf16[1024,2048]{1,0:T(8,128)(2,1)} async-done(((bf16[128,2048]{1,0:T(8,128)(2,1)}), bf16[1024,2048]{1,0:T(8,128)(2,1)}) %all-gather.11.cloned.1.call-update) | async-done | bytes 4194320 | tf_op jit(solution)/shard_map/all_gather | solution.py:138
  440.0 8.2 %fusion.49 = f32[1024,768]{1,0:T(8,128)} fusion(bf16[1024,2048]{1,0:T(8,128)(2,1)} %all-gather.11.cloned.1.call-done, bf16[2048,768]{1,0:T(8,128)(2,1)} %bitcast.100), kind=kOutput, calls=%fused_computation.91 | convolution fusion | flops 3221225472 | bytes 10485760 | tf_op jit(solution)/shard_map/dot_general | solution.py:139
  448.2 12.2 %convolution_convert_fusion.1 = bf16[1024,2048]{1,0:T(8,128)(2,1)} fusion(bf16[768,2048]{0,1:T(8,128)(2,1)} %bitcast.101, f32[1024,768]{1,0:T(8,128)} %fusion.49, bf16[1024,2048]{1,0:T(8,128)(2,1)} %all-gather.11.cloned.1.call-done, bf16[2048,768]{1,0:T(8,128)(2,1)S(1)} %bitcast.99), kind=kOutput, calls=%fused_computation.22 | convolution fusion | flops 6449266688 | bytes 17825792 | tf_op jit(solution)/shard_map/dot_general | solution.py:142
  460.5 0.9 copy-done.6
  461.4 1.9 pad_maximum_fusion
  463.3 49.1 %reduce-scatter.5.cloned.1.call-done = bf16[128,2048]{1,0:T(8,128)(2,1)} async-done(((bf16[1024,2048]{1,0:T(8,128)(2,1)}), bf16[128,2048]{1,0:T(8,128)(2,1)}) %reduce-scatter.5.cloned.1.call-update) | async-done | bytes 524304 | tf_op jit(solution)/shard_map/reduce_scatter | solution.py:143
  512.4 2.0 fusion.20
  (60 shorter events, 0.5 us)
Async XLA Ops:
  7.2 6.5 %copy-start.10 = (f32[128,128]{1,0:T(8,128)S(1)}, f32[128,128]{1,0:T(8,128)}, u32[]{:S(2)}) copy-start(f32[128,128]{1,0:T(8,128)} %param.22) | copy-start | bytes 196612
  7.2 6.6 %copy-start.14 = (f32[2048]{0:T(1024)S(1)}, f32[2048]{0:T(1024)}, u32[]{:S(2)}) copy-start(f32[2048]{0:T(1024)} %param.17) | copy-start | bytes 24580
  7.2 86.1 %all-gather.7.cloned.1.call-start = ((), (), s32[]{:S(2)}) async-start(), calls=%async_computation.5 | async-start | bytes 1114112 | tf_op jit(solution)/shard_map/all_gather | solution.py:54
  8.8 110.9 %all-gather.9.cloned.1.call-start = ((), (), s32[]{:S(2)}) async-start(), calls=%async_computation.6 | async-start | bytes 1114112 | tf_op jit(solution)/shard_map/all_gather | solution.py:113
  10.4 146.6 %all-gather.13.cloned.1.call-start = ((), (), s32[]{:S(2)}) async-start(), calls=%async_computation.9 | async-start | bytes 3342336 | tf_op jit(solution)/shard_map/all_gather | solution.py:129
  10.4 3.5 copy-start
  14.9 30.5 %copy-start.1 = (bf16[1024,2048]{1,0:T(8,128)(2,1)}, bf16[1024,2048]{1,0:T(8,128)(2,1)S(1)}, u32[]{:S(2)}) copy-start(bf16[1024,2048]{1,0:T(8,128)(2,1)S(1)} %fusion.2) | copy-start | bytes 12582916
  14.9 32.2 %copy-start.12 = (s32[1024]{0:T(1024)S(1)}, s32[1024]{0:T(1024)}, u32[]{:S(2)}) copy-start(s32[1024]{0:T(1024)} %param.16) | copy-start | bytes 12292
  15.0 32.2 %copy-start.16 = (f32[128]{0:T(128)S(1)}, f32[128]{0:T(128)}, u32[]{:S(2)}) copy-start(f32[128]{0:T(128)} %param.20) | copy-start | bytes 1540
  45.4 7.9 %copy-start.11 = (f32[128,128]{1,0:T(8,128)S(1)}, f32[128,128]{1,0:T(8,128)}, u32[]{:S(2)}) copy-start(f32[128,128]{1,0:T(8,128)} %param.23) | copy-start | bytes 196612
  49.8 0.7 copy-start.4
  49.8 34.6 %copy-start.7 = (f32[256,384]{1,0:T(8,128)S(1)}, f32[256,384]{1,0:T(8,128)}, u32[]{:S(2)}) copy-start(f32[256,384]{1,0:T(8,128)} %param.25) | copy-start | bytes 1179652
  50.5 35.0 %copy-start.13 = (s32[1024]{0:T(1024)S(1)}, s32[1024]{0:T(1024)}, u32[]{:S(2)}) copy-start(s32[1024]{0:T(1024)} %param.15) | copy-start | bytes 12292
  51.4 50.4 %collective-permute-start.1 = (bf16[1024,128]{1,0:T(8,128)(2,1)}, bf16[1024,128]{1,0:T(8,128)(2,1)}, u32[]{:S(2)}, u32[]{:S(2)}) collective-permute-start(bf16[1024,128]{1,0:T(8,128)(2,1)} %pad_maximum_fusion.3), channel_id=1, source_target_pairs={{0,8},{8,16},{16,24},{24,32},{32,40},{40,48},{48,56},{56,64},{64,7... | collective-permute-start | bytes 786440 | tf_op jit(solution)/shard_map/ppermute | solution.py:13
  80.9 31.0 %collective-permute-start = (bf16[1024,128]{1,0:T(8,128)(2,1)}, bf16[1024,128]{1,0:T(8,128)(2,1)}, u32[]{:S(2)}, u32[]{:S(2)}) collective-permute-start(bf16[1024,128]{1,0:T(8,128)(2,1)} %convolution_convert_fusion.2), channel_id=1, source_target_pairs={{0,8},{8,16},{16,24},{24,32},{32,40},{40,48},{48,56},{56,64},{64,7... | collective-permute-start | bytes 786440 | tf_op jit(solution)/shard_map/ppermute | solution.py:13
  85.2 157.4 %reduce-scatter.3.cloned.1.call-start = ((), (), s32[]{:S(2)}) async-start(), calls=%async_computation.7 | async-start | bytes 4718592 | tf_op jit(solution)/shard_map/reduce_scatter | solution.py:116
  93.3 6.5 %copy-start.17 = (f32[128]{0:T(128)S(1)}, f32[128]{0:T(128)}, u32[]{:S(2)}) copy-start(f32[128]{0:T(128)} %param.19) | copy-start | bytes 1540
  99.7 2.1 copy-start.5
  119.7 4.6 copy-start.8
  124.2 1.0 copy-start.9
  124.2 170.8 %all-gather.15.cloned.1.call-start = ((), (), s32[]{:S(2)}) async-start(), calls=%async_computation.10 | async-start | bytes 3342336 | tf_op jit(solution)/shard_map/all_gather | solution.py:130
  125.1 229.1 %all-gather.17.cloned.1.call-start = ((), (), s32[]{:S(2)}) async-start(), calls=%async_computation.11 | async-start | bytes 3342336 | tf_op jit(solution)/shard_map/all_gather | solution.py:132
  157.0 87.7 %copy-start.15 = (f32[2048]{0:T(1024)S(1)}, f32[2048]{0:T(1024)}, u32[]{:S(2)}) copy-start(f32[2048]{0:T(1024)} %param.18) | copy-start | bytes 24580
  157.0 138.0 %all-to-all-start = ((bf16[256,8,768]{0,2,1:T(8,128)(2,1)}), bf16[256,8,768]{0,2,1:T(8,128)(2,1)S(1)}, u32[]{:S(2)}, u32[]{:S(2)}) async-start(bf16[256,8,768]{0,2,1:T(8,128)(2,1)} %bitcast.96), calls=%async_computation.1 | async-start | bytes 6291456 | tf_op jit(solution)/shard_map/all_to_all | solution.py:134
  161.2 278.8 %all-gather.11.cloned.1.call-start = ((), (), s32[]{:S(2)}) async-start(), calls=%async_computation.8 | async-start | bytes 4718592 | tf_op jit(solution)/shard_map/all_gather | solution.py:138
  243.9 0.8 copy-start.2
  295.0 59.3 %all-to-all-start.1 = ((bf16[256,8,768]{0,2,1:T(8,128)(2,1)}), bf16[256,8,768]{0,2,1:T(8,128)(2,1)}, u32[]{:S(2)}, u32[]{:S(2)}) async-start(bf16[256,8,768]{0,2,1:T(8,128)(2,1)} %bitcast.98), calls=%async_computation.2 | async-start | bytes 6291456 | tf_op jit(solution)/shard_map/all_to_all | solution.py:135
  354.2 65.3 %all-to-all-start.2 = ((bf16[8,768,256]{2,1,0:T(8,128)(2,1)}), bf16[8,768,256]{2,1,0:T(8,128)(2,1)}, u32[]{:S(2)}, u32[]{:S(2)}) async-start(bf16[8,768,256]{2,1,0:T(8,128)(2,1)} %bitcast.97), calls=%async_computation.3 | async-start | bytes 6291456 | tf_op jit(solution)/shard_map/all_to_all | solution.py:137
  358.8 153.6 %reduce-scatter.5.cloned.1.call-start = ((), (), s32[]{:S(2)}) async-start(), calls=%async_computation.12 | async-start | bytes 4718592 | tf_op jit(solution)/shard_map/reduce_scatter | solution.py:143
  460.4 0.9 copy-start.6
  460.4 52.0 %copy-start.3 = (bf16[128,2048]{1,0:T(8,128)(2,1)S(1)}, bf16[128,2048]{1,0:T(8,128)(2,1)}, u32[]{:S(2)}) copy-start(bf16[128,2048]{1,0:T(8,128)(2,1)} %copy-done.2) | copy-start | bytes 1572868
Sparse Core Ops, SparseCore 0:
  10.5 48.5 all-gather.6
  61.5 42.2 all-gather.8
  106.2 50.8 all-gather.12
  159.3 83.2 reduce-scatter.2
  244.9 50.0 all-gather.14
  297.3 56.8 all-gather.16
  356.5 83.5 all-gather.10
  460.6 51.7 reduce-scatter.4
where the time goes:
time: 522 us; the launch traced here: 521 us
  waiting for transfers between devices  336 us (64%)
  blocking collectives  53.9 us (10%)
  matrix products  49.1 us (9%)
  other arithmetic  30.2 us (6%)
  starting transfers between devices  19.1 us (4%)
  local copies, waits for them, and re-layouts  17.9 us (3%)
  between operations  15.1 us (3%)
    reduce_scatter x1, waiting for transfers between devices, per_device(): lax.psum_scatter(head_terms.astype(jnp.bfloat16), 'mdl', scatter_dimensio...  81.4 us
    all_gather x1, waiting for transfers between devices, per_device(): down_whole = lax.all_gather(down_local, 'req', axis=0, tiled=True)  54.8 us
    all_to_all x1, waiting for transfers between devices, per_device(): lax.all_to_all(down_whole, 'mdl', split_axis=0, concat_axis=1, tiled=True)  54.4 us
    all_gather x1, waiting for transfers between devices, per_device(): lax.all_gather(up_local, 'req', axis=1, tiled=True)  49.2 us
    reduce_scatter x1, waiting for transfers between devices, per_device(): lax.psum_scatter(unit_terms.astype(jnp.bfloat16), 'mdl', scatter_dimensio...  49.1 us
    all_gather x1, waiting for transfers between devices, per_device(): lax.all_gather(gate_local, 'req', axis=1, tiled=True)  31.1 us
    all_gather x1, blocking collectives, per_device(): lax.all_gather(key_matrix.astype(jnp.bfloat16), 'req', axis=0, tiled=True)  30.4 us
    all_gather x1, blocking collectives, per_device(): lax.all_gather(value_matrix.astype(jnp.bfloat16), 'req', axis=0, tiled=True)  23.4 us
  transfers between devices with their start and end apart: 13, of which 7 were waited for; matrix products, arithmetic and copies ran while one was open for 14% of the time, Pallas kernels for 0%

commit v1 on v0

--- a/solution.py
+++ b/solution.py
@@ -134,7 +134,9 @@
         lax.all_to_all(gate_whole, "mdl", split_axis=1, concat_axis=0, tiled=True),
         lax.all_to_all(up_whole, "mdl", split_axis=1, concat_axis=0, tiled=True),
     )
-    down_server = lax.all_to_all(down_whole, "mdl", split_axis=0, concat_axis=1, tiled=True)
+    parts = jnp.split(down_whole, lax.axis_size("mdl"), axis=0)
+    received = lax.all_to_all(jnp.stack(parts), "mdl", 0, 0)
+    down_server = jnp.concatenate(received, axis=1)
     piece = lax.all_gather(mlp_in, "mdl", axis=0, tiled=True)
     gate = jnp.dot(piece, gate_server, preferred_element_type=jnp.float32)
     upper = jnp.dot(piece, up_server, preferred_element_type=jnp.float32)

time: 522 us -> 532 us (1.019)
  local copies, waits for them, and re-layouts: 17.9 us -> 28.1 us
    all_to_all x1, waiting for transfers between devices: 54.4 us -> 0.01 us  [per_device(): received = lax.all_to_all(jnp.stack(parts), 'mdl', 0, 0)]
    all_gather x1, waiting for transfers between devices: 15.7 us -> 66.9 us  [per_device(): piece = lax.all_gather(mlp_in, 'mdl', axis=0, tiled=True)]
    unnamed x38 -> x46, local copies, waits for them, and re-layouts: 4.06 us -> 17.3 us
  transfers between devices with their start and end apart: 13 -> 13, of which waited for: 7 -> 6; matrix products, arithmetic and copies ran while one was open for 14% -> 17% of each run, Pallas kernels for 0% -> 0%
where the time goes in v1:
time: 532 us; the launch traced here: 531 us
  waiting for transfers between devices  336 us (63%)
  blocking collectives  53.9 us (10%)
  matrix products  49.3 us (9%)
  other arithmetic  29.5 us (6%)
  local copies, waits for them, and re-layouts  28.1 us (5%)
  starting transfers between devices  19.2 us (4%)
  between operations  15.2 us (3%)
    reduce_scatter x1, waiting for transfers between devices, per_device(): lax.psum_scatter(head_terms.astype(jnp.bfloat16), 'mdl', scatter_dimensio...  81.4 us
    all_gather x1, waiting for transfers between devices, per_device(): piece = lax.all_gather(mlp_in, 'mdl', axis=0, tiled=True)  66.9 us
    all_gather x1, waiting for transfers between devices, per_device(): down_whole = lax.all_gather(down_local, 'req', axis=0, tiled=True)  55.4 us
    reduce_scatter x1, waiting for transfers between devices, per_device(): lax.psum_scatter(unit_terms.astype(jnp.bfloat16), 'mdl', scatter_dimensio...  51.7 us
    all_gather x1, waiting for transfers between devices, per_device(): lax.all_gather(up_local, 'req', axis=1, tiled=True)  49.2 us
    all_gather x1, waiting for transfers between devices, per_device(): lax.all_gather(gate_local, 'req', axis=1, tiled=True)  30.9 us
    all_gather x1, blocking collectives, per_device(): lax.all_gather(key_matrix.astype(jnp.bfloat16), 'req', axis=0, tiled=True)  30.5 us
    all_gather x1, blocking collectives, per_device(): lax.all_gather(value_matrix.astype(jnp.bfloat16), 'req', axis=0, tiled=True)  23.4 us
  transfers between devices with their start and end apart: 13, of which 6 were waited for; matrix products, arithmetic and copies ran while one was open for 17% of the time, Pallas kernels for 0%

profile of v1, /device:TPU:1, one launch (start us, length us, event | category | flops | bytes accessed | tf_op | source)
XLA Modules:
  0.0 530.7 jit_solution(4713531751264445141)
XLA Ops:
  7.2 1.5 convert_element_type.107
  8.8 1.5 convert_element_type.116
  10.5 3.2 fusion
  13.9 1.0 fusion.2
  15.0 30.5 %all_gather.25 = bf16[2048,128]{1,0:T(8,128)(2,1)S(1)} all-gather(bf16[128,128]{1,0:T(8,128)(2,1)S(1)} %convert_element_type.105), channel_id=1, replica_groups=mesh['req'=16,'mdl'=8] {'req'}, dimensions={0}, use_global_device_ids=true | all-gather | bytes 557056 | tf_op jit(solution)/shard_map/all_gather | solution.py:55
  45.4 1.5 multiply_reduce_fusion.1
  47.0 0.2 copy.29
  47.2 0.2 multiply_bitcast_fusion
  47.4 2.4 fusion.26
  49.9 0.7 copy-done.4
  50.6 0.9 pad_maximum_fusion.3
  51.4 1.9 collective-permute-start.1
  53.4 23.4 %all_gather.24 = bf16[2048,128]{1,0:T(8,128)(2,1)S(1)} all-gather(bf16[128,128]{1,0:T(8,128)(2,1)S(1)} %convert_element_type.103), channel_id=1, replica_groups=mesh['req'=16,'mdl'=8] {'req'}, dimensions={0}, use_global_device_ids=true | all-gather | bytes 557056 | tf_op jit(solution)/shard_map/all_gather | solution.py:56
  76.7 4.1 convolution_convert_fusion.2
  80.9 3.6 collective-permute-start
  84.5 0.8 copy.35
  85.3 0.2 reduce-scatter.3.cloned.1.call-start
  85.6 0.5 slice.40
  86.1 0.5 slice.41
  86.6 3.0 multiply_cosine_fusion
  89.6 0.6 broadcast_compare_fusion.1
  90.9 0.5 broadcast_and_fusion.1
  91.4 1.2 compare_and_fusion.1
  92.6 0.8 pad_add_fusion
  93.4 4.8 multiply_reduce_fusion
  98.3 1.5 copy.30
  99.9 0.3 multiply_multiply_fusion
  100.2 1.7 subtract_convert_fusion
  101.9 2.9 fusion.5
  104.8 2.9 fusion.6
  107.8 2.0 fusion.3
  109.8 2.2 fusion.4
  112.0 3.9 fusion.11
  115.9 3.9 fusion.14
  119.8 4.5 convolution_convert_fusion
  124.4 0.8 copy.37
  125.3 0.8 copy.39
  126.2 30.9 %all-gather.13.cloned.1.call-done = bf16[256,6144]{0,1:T(8,128)(2,1)} async-done(((bf16[256,384]{0,1:T(8,128)(2,1)}), bf16[256,6144]{0,1:T(8,128)(2,1)}) %all-gather.13.cloned.1.call-update) | async-done | bytes 3145744 | tf_op jit(solution)/shard_map/all_gather | solution.py:129
  157.1 4.1 all-to-all-start
  161.3 81.4 %reduce-scatter.3.cloned.1.call-done = bf16[128,2048]{1,0:T(8,128)(2,1)} async-done(((bf16[1024,2048]{1,0:T(8,128)(2,1)}), bf16[128,2048]{1,0:T(8,128)(2,1)}) %reduce-scatter.3.cloned.1.call-update) | async-done | bytes 524304 | tf_op jit(solution)/shard_map/reduce_scatter | solution.py:116
  242.6 1.3 add_convert_fusion
  244.2 0.6 copy-done.2
  244.8 1.0 fusion.19
  245.8 49.2 %all-gather.15.cloned.1.call-done = bf16[256,6144]{0,1:T(8,128)(2,1)} async-done(((bf16[256,384]{0,1:T(8,128)(2,1)}), bf16[256,6144]{0,1:T(8,128)(2,1)}) %all-gather.15.cloned.1.call-update) | async-done | bytes 3145744 | tf_op jit(solution)/shard_map/all_gather | solution.py:130
  295.0 4.5 all-to-all-start.1
  299.5 55.4 %all-gather.17.cloned.1.call-done = bf16[6144,256]{0,1:T(8,128)(2,1)} async-done(((bf16[384,256]{0,1:T(8,128)(2,1)}), bf16[6144,256]{0,1:T(8,128)(2,1)}) %all-gather.17.cloned.1.call-update) | async-done | bytes 3145744 | tf_op jit(solution)/shard_map/all_gather | solution.py:132
  354.9 1.8 fusion.39
  356.6 1.8 fusion.38
  358.4 1.8 fusion.37
  360.2 1.8 fusion.36
  362.0 1.8 fusion.35
  363.7 1.8 fusion.34
  365.5 1.8 fusion.33
  367.3 1.8 fusion.32
  369.0 4.6 all-to-all-start.2
  373.7 3.1 copy.36
  376.8 3.2 copy.38
  379.9 66.9 %all-gather.11.cloned.1.call-done = bf16[1024,2048]{1,0:T(8,128)(2,1)} async-done(((bf16[128,2048]{1,0:T(8,128)(2,1)}), bf16[1024,2048]{1,0:T(8,128)(2,1)}) %all-gather.11.cloned.1.call-update) | async-done | bytes 4194320 | tf_op jit(solution)/shard_map/all_gather | solution.py:140
  446.8 8.2 %fusion.57 = f32[1024,768]{1,0:T(8,128)} fusion(bf16[1024,2048]{1,0:T(8,128)(2,1)} %all-gather.11.cloned.1.call-done, bf16[2048,768]{1,0:T(8,128)(2,1)} %bitcast.131), kind=kOutput, calls=%fused_computation.107 | convolution fusion | flops 3221225472 | bytes 10485760 | tf_op jit(solution)/shard_map/dot_general | solution.py:141
  455.1 12.3 %convolution_convert_fusion.1 = bf16[1024,2048]{1,0:T(8,128)(2,1)} fusion(bf16[768,2048]{0,1:T(8,128)(2,1)} %bitcast.36, f32[1024,768]{1,0:T(8,128)} %fusion.57, bf16[1024,2048]{1,0:T(8,128)(2,1)} %all-gather.11.cloned.1.call-done, bf16[2048,768]{1,0:T(8,128)(2,1)S(1)} %bitcast.130), kind=kOutput, calls=%fused_computation.22 | convolution fusion | flops 6449266688 | bytes 17825792 | tf_op jit(solution)/shard_map/dot_general | solution.py:144
  467.4 0.9 copy-done.6
  468.3 1.9 pad_maximum_fusion
  470.2 51.7 %reduce-scatter.5.cloned.1.call-done = bf16[128,2048]{1,0:T(8,128)(2,1)} async-done(((bf16[1024,2048]{1,0:T(8,128)(2,1)}), bf16[128,2048]{1,0:T(8,128)(2,1)}) %reduce-scatter.5.cloned.1.call-update) | async-done | bytes 524304 | tf_op jit(solution)/shard_map/reduce_scatter | solution.py:145
  521.9 2.0 fusion.20
  (67 shorter events, 1.0 us)
Async XLA Ops:
  7.2 6.5 %copy-start.10 = (f32[128,128]{1,0:T(8,128)S(1)}, f32[128,128]{1,0:T(8,128)}, u32[]{:S(2)}) copy-start(f32[128,128]{1,0:T(8,128)} %param.22) | copy-start | bytes 196612
  7.2 6.5 %copy-start.14 = (f32[2048]{0:T(1024)S(1)}, f32[2048]{0:T(1024)}, u32[]{:S(2)}) copy-start(f32[2048]{0:T(1024)} %param.17) | copy-start | bytes 24580
  7.2 86.2 %all-gather.7.cloned.1.call-start = ((), (), s32[]{:S(2)}) async-start(), calls=%async_computation.5 | async-start | bytes 1114112 | tf_op jit(solution)/shard_map/all_gather | solution.py:54
  8.8 111.0 %all-gather.9.cloned.1.call-start = ((), (), s32[]{:S(2)}) async-start(), calls=%async_computation.6 | async-start | bytes 1114112 | tf_op jit(solution)/shard_map/all_gather | solution.py:113
  10.4 146.7 %all-gather.13.cloned.1.call-start = ((), (), s32[]{:S(2)}) async-start(), calls=%async_computation.9 | async-start | bytes 3342336 | tf_op jit(solution)/shard_map/all_gather | solution.py:129
  10.4 3.5 copy-start
  14.9 30.5 %copy-start.1 = (bf16[1024,2048]{1,0:T(8,128)(2,1)}, bf16[1024,2048]{1,0:T(8,128)(2,1)S(1)}, u32[]{:S(2)}) copy-start(bf16[1024,2048]{1,0:T(8,128)(2,1)S(1)} %fusion.2) | copy-start | bytes 12582916
  14.9 32.3 %copy-start.12 = (s32[1024]{0:T(1024)S(1)}, s32[1024]{0:T(1024)}, u32[]{:S(2)}) copy-start(s32[1024]{0:T(1024)} %param.16) | copy-start | bytes 12292
  14.9 32.3 %copy-start.16 = (f32[128]{0:T(128)S(1)}, f32[128]{0:T(128)}, u32[]{:S(2)}) copy-start(f32[128]{0:T(128)} %param.20) | copy-start | bytes 1540
  45.4 7.9 %copy-start.11 = (f32[128,128]{1,0:T(8,128)S(1)}, f32[128,128]{1,0:T(8,128)}, u32[]{:S(2)}) copy-start(f32[128,128]{1,0:T(8,128)} %param.23) | copy-start | bytes 196612
  49.9 0.7 copy-start.4
  49.9 34.6 %copy-start.7 = (f32[256,384]{1,0:T(8,128)S(1)}, f32[256,384]{1,0:T(8,128)}, u32[]{:S(2)}) copy-start(f32[256,384]{1,0:T(8,128)} %param.25) | copy-start | bytes 1179652
  50.6 35.0 %copy-start.13 = (s32[1024]{0:T(1024)S(1)}, s32[1024]{0:T(1024)}, u32[]{:S(2)}) copy-start(s32[1024]{0:T(1024)} %param.15) | copy-start | bytes 12292
  51.4 50.4 %collective-permute-start.1 = (bf16[1024,128]{1,0:T(8,128)(2,1)}, bf16[1024,128]{1,0:T(8,128)(2,1)}, u32[]{:S(2)}, u32[]{:S(2)}) collective-permute-start(bf16[1024,128]{1,0:T(8,128)(2,1)} %pad_maximum_fusion.3), channel_id=1, source_target_pairs={{0,8},{8,16},{16,24},{24,32},{32,40},{40,48},{48,56},{56,64},{64,7... | collective-permute-start | bytes 786440 | tf_op jit(solution)/shard_map/ppermute | solution.py:13
  80.9 31.1 %collective-permute-start = (bf16[1024,128]{1,0:T(8,128)(2,1)}, bf16[1024,128]{1,0:T(8,128)(2,1)}, u32[]{:S(2)}, u32[]{:S(2)}) collective-permute-start(bf16[1024,128]{1,0:T(8,128)(2,1)} %convolution_convert_fusion.2), channel_id=1, source_target_pairs={{0,8},{8,16},{16,24},{24,32},{32,40},{40,48},{48,56},{56,64},{64,7... | collective-permute-start | bytes 786440 | tf_op jit(solution)/shard_map/ppermute | solution.py:13
  85.3 157.3 %reduce-scatter.3.cloned.1.call-start = ((), (), s32[]{:S(2)}) async-start(), calls=%async_computation.7 | async-start | bytes 4718592 | tf_op jit(solution)/shard_map/reduce_scatter | solution.py:116
  93.4 6.5 %copy-start.17 = (f32[128]{0:T(128)S(1)}, f32[128]{0:T(128)}, u32[]{:S(2)}) copy-start(f32[128]{0:T(128)} %param.19) | copy-start | bytes 1540
  99.8 2.1 copy-start.5
  119.8 4.6 copy-start.8
  124.3 1.0 copy-start.9
  124.4 170.6 %all-gather.15.cloned.1.call-start = ((), (), s32[]{:S(2)}) async-start(), calls=%async_computation.10 | async-start | bytes 3342336 | tf_op jit(solution)/shard_map/all_gather | solution.py:130
  125.3 229.6 %all-gather.17.cloned.1.call-start = ((), (), s32[]{:S(2)}) async-start(), calls=%async_computation.11 | async-start | bytes 3342336 | tf_op jit(solution)/shard_map/all_gather | solution.py:132
  157.1 87.7 %copy-start.15 = (f32[2048]{0:T(1024)S(1)}, f32[2048]{0:T(1024)}, u32[]{:S(2)}) copy-start(f32[2048]{0:T(1024)} %param.18) | copy-start | bytes 24580
  157.1 138.0 %all-to-all-start = ((bf16[256,8,768]{0,2,1:T(8,128)(2,1)}), bf16[256,8,768]{0,2,1:T(8,128)(2,1)S(1)}, u32[]{:S(2)}, u32[]{:S(2)}) async-start(bf16[256,8,768]{0,2,1:T(8,128)(2,1)} %bitcast.128), calls=%async_computation.1 | async-start | bytes 6291456 | tf_op jit(solution)/shard_map/all_to_all | solution.py:134
  161.2 285.6 %all-gather.11.cloned.1.call-start = ((), (), s32[]{:S(2)}) async-start(), calls=%async_computation.8 | async-start | bytes 4718592 | tf_op jit(solution)/shard_map/all_gather | solution.py:140
  244.0 0.8 copy-start.2
  295.0 74.0 %all-to-all-start.1 = ((bf16[256,8,768]{0,2,1:T(8,128)(2,1)}), bf16[256,8,768]{0,2,1:T(8,128)(2,1)}, u32[]{:S(2)}, u32[]{:S(2)}) async-start(bf16[256,8,768]{0,2,1:T(8,128)(2,1)} %bitcast.129), calls=%async_computation.2 | async-start | bytes 6291456 | tf_op jit(solution)/shard_map/all_to_all | solution.py:135
  369.0 86.0 %all-to-all-start.2 = ((bf16[8,768,256]{1,2,0:T(8,128)(2,1)}), bf16[8,768,256]{1,2,0:T(8,128)(2,1)}, u32[]{:S(2)}, u32[]{:S(2)}) async-start(bf16[8,768,256]{1,2,0:T(8,128)(2,1)} %fusion.32), calls=%async_computation.3 | async-start | bytes 6291456 | tf_op jit(solution)/shard_map/all_to_all | solution.py:138
  373.6 148.3 %reduce-scatter.5.cloned.1.call-start = ((), (), s32[]{:S(2)}) async-start(), calls=%async_computation.12 | async-start | bytes 4718592 | tf_op jit(solution)/shard_map/reduce_scatter | solution.py:145
  467.4 0.9 copy-start.6
  467.4 54.5 %copy-start.3 = (bf16[128,2048]{1,0:T(8,128)(2,1)S(1)}, bf16[128,2048]{1,0:T(8,128)(2,1)}, u32[]{:S(2)}) copy-start(bf16[128,2048]{1,0:T(8,128)(2,1)} %copy-done.2) | copy-start | bytes 1572868
Sparse Core Ops, SparseCore 0:
  10.5 48.5 all-gather.6
  61.5 42.2 all-gather.8
  106.2 50.8 all-gather.12
  159.3 83.2 reduce-scatter.2
  244.9 50.0 all-gather.14
  297.2 57.6 all-gather.16
  357.1 89.6 all-gather.10
  467.5 54.3 reduce-scatter.4
